TPU v7x, 32 devices: a whole 2x2x4 slice. The times are simulated.
32 devices in a mesh: phase: 4 (over x, core), seq: 4 (over z), mp: 2 (over y).
Axes of the slice: x: 2, y: 2, z: 4, core: 2. Of those that a mesh axis runs over, the one named last changes fastest.
Arguments:
- queries: bfloat16 [4, 2048, 4096], P('phase', 'seq', 'mp'), may hold values from -360 to 360
- key_weight: bfloat16 [4, 1024, 4096], P('phase', None, 'mp'), may hold values from -0.1875 to 0.1875
- value_weight: bfloat16 [4, 1024, 4096], P('phase', None, 'mp'), may hold values from -0.1875 to 0.1875
- enc_gain: float32 [1024], replicated, may hold values from 0.25 to 2
- neighbour_states: bfloat16 [80, 64, 1024], P('seq', ('phase', 'mp')), may hold values from -600 to 600
- slot_dest: int32 [80], P('seq'), may hold values from -1 to 63, as said below
Outputs:
- context: bfloat16 [4, 2048, 4096], P('phase', 'seq', 'mp')
Inputs may be any that keep to these rules, and one draw needn't show every extreme that they name: slot_dest names every position 0 to 63 exactly once and is -1 elsewhere. Positions 2 * 8 j to 2 * 8 (j + 1) - 1 belong to the tokens of index j of seq. The slots of one index of seq name at most 5 positions of any one index of seq, and this bound is reached; one index of seq has up to 20 filled slots, reached in every draw.
All inputs are finite; a program needn't handle non-finite values.
Results may differ from a plain program's by a relative error of at most 0.0074.
Values may be sent and summed in bfloat16 or wider, within the bound.
No kernel may reach another device: no remote copies, remote signals or barrier semaphores. Data moves between devices by JAX's collectives and lax.ppermute only.
A program may use at most 64 MiB of HBM per device.

v0:
```python
import jax
import jax.numpy as jnp
from jax import lax
from jax.sharding import PartitionSpec as P

HD = 128
SEGLEN = 64
NLEN = 64
NEIGH = 2


def shifted(shard, axis, by):
    peers = lax.axis_size(axis)
    pairs = [(i, i + by) for i in range(peers) if 0 <= i + by < peers]
    return lax.ppermute(shard, axis, pairs)


def normalize(rows, gain):
    states = rows.astype(jnp.float32)
    meansq = jnp.mean(states * states, axis=-1, keepdims=True)
    return (states * lax.rsqrt(meansq + 1e-06) * gain).astype(jnp.bfloat16)


def project(rows, weight):
    flattened = rows.reshape(-1, rows.shape[-1])
    return jnp.dot(flattened, weight, preferred_element_type=jnp.float32).astype(jnp.bfloat16)


def attend(query_win, key_win, value_win):
    windows = query_win.shape[0]
    heads = query_win.shape[2] // HD
    query_four = query_win.reshape(windows, query_win.shape[1], heads, HD)
    key_four = key_win.reshape(windows, key_win.shape[1], heads, HD)
    value_four = value_win.reshape(windows, value_win.shape[1], heads, HD)
    scores = jnp.einsum(
        "wqhd,wkhd->whqk", query_four, key_four, preferred_element_type=jnp.float32
    ) * HD ** (-0.5)
    top = jnp.max(scores, axis=-1, keepdims=True)
    exponent = jnp.exp(scores - top)
    weights = (exponent / jnp.sum(exponent, axis=-1, keepdims=True)).astype(jnp.bfloat16)
    context = jnp.einsum("whqk,wkhd->wqhd", weights, value_four, preferred_element_type=jnp.float32)
    return context.astype(jnp.bfloat16).reshape(windows, query_win.shape[1], heads * HD)


def packing(slot_dest, shards, per_shard, capacity):
    count = slot_dest.shape[0]
    is_live = slot_dest >= 0
    target = jnp.where(is_live, slot_dest // per_shard, -1)
    order = jnp.arange(count)
    earlier = (target[:, None] == target[None, :]) & (order[None, :] < order[:, None])
    slot_rank = jnp.sum(earlier.astype(jnp.int32), axis=1)
    buffer_slot = jnp.where(is_live, target * capacity + slot_rank, -1)
    matches = jnp.arange(shards * capacity)[:, None] == buffer_slot[None, :]
    selector = matches.astype(jnp.bfloat16)
    sent_dest = jnp.sum(jnp.where(matches, slot_dest[None, :] + 1, 0), axis=1) - 1
    return (selector, sent_dest.reshape(shards, capacity))


def pack(selector, rows, shards, capacity):
    flattened = rows.reshape(rows.shape[0], rows.shape[1] * rows.shape[2])
    packed = jnp.dot(selector, flattened, preferred_element_type=jnp.float32).astype(jnp.bfloat16)
    return packed.reshape(shards, capacity, rows.shape[1], rows.shape[2])


def unpack(received, received_dest, own_index, per_shard):
    flat_dest = received_dest.reshape(-1)
    local = jnp.where(flat_dest >= 0, flat_dest - own_index * per_shard, -1)
    placer = (jnp.arange(per_shard)[:, None] == local[None, :]).astype(jnp.bfloat16)
    stacked = received.reshape(flat_dest.shape[0], received.shape[2] * received.shape[3])
    placed = jnp.dot(placer, stacked, preferred_element_type=jnp.float32).astype(jnp.bfloat16)
    return placed.reshape(per_shard, received.shape[2], received.shape[3])


def edge_windows(query_rows, keys, values, prev_keys, prev_values):
    tokens_here = query_rows.shape[0]
    width = query_rows.shape[1]
    blocks = keys.shape[0]
    padded = jnp.concatenate(
        [
            jnp.zeros((1, width), jnp.bfloat16),
            query_rows,
            jnp.zeros((SEGLEN - 1, width), jnp.bfloat16),
        ],
        axis=0,
    )
    padded = padded.reshape(blocks + 1, SEGLEN, width)
    all_keys = jnp.concatenate([prev_keys[None], keys], axis=0)
    all_values = jnp.concatenate([prev_values[None], values], axis=0)
    context = attend(padded, all_keys, all_values)
    return context.reshape((blocks + 1) * SEGLEN, width)[1 : tokens_here + 1]


def on_device(queries, key_weight, value_weight, enc_gain, neighbour_states, slot_dest):
    shards = lax.axis_size("seq")
    own_index = lax.axis_index("seq")
    query_rows = queries[0]
    tokens_here = query_rows.shape[0]
    blocks = tokens_here // SEGLEN
    per_shard = NEIGH * blocks
    capacity = per_shard // shards + 1
    selector, sent_dest = packing(slot_dest, shards, per_shard, capacity)
    received, received_dest = (
        lax.all_to_all(
            pack(selector, neighbour_states, shards, capacity),
            "seq",
            split_axis=0,
            concat_axis=0,
            tiled=True,
        ),
        lax.all_to_all(sent_dest, "seq", split_axis=0, concat_axis=0, tiled=True),
    )
    arranged = unpack(received, received_dest, own_index, per_shard)
    routed = lax.all_gather(arranged, ("phase", "mp"), axis=1, tiled=True)
    neighbours = normalize(routed, enc_gain)
    key_mat = key_weight[0]
    value_mat = value_weight[0]
    width = key_mat.shape[1]
    keys = project(neighbours, key_mat).reshape(blocks, NEIGH * NLEN, width)
    values = project(neighbours, value_mat).reshape(blocks, NEIGH * NLEN, width)
    prev_keys, prev_values = shifted((keys[blocks - 1], values[blocks - 1]), "seq", 1)
    joined = edge_windows(query_rows, keys, values, prev_keys, prev_values)
    position = jnp.arange(tokens_here) + 1
    window_index = own_index * blocks + position // SEGLEN
    silent = (position % SEGLEN != 0) & (window_index == 0)
    result = jnp.where(silent[:, None], jnp.zeros_like(joined), joined)
    return result[None]


def solution(mesh):
    in_specs = (
        P("phase", "seq", "mp"),
        P("phase", None, "mp"),
        P("phase", None, "mp"),
        P(),
        P("seq", ("phase", "mp"), None),
        P("seq"),
    )
    out_specs = P("phase", "seq", "mp")
    return jax.shard_map(
        on_device, mesh=mesh, in_specs=in_specs, out_specs=out_specs, check_vma=False
    )
```

profile of v0, /device:TPU:0, one launch (start us, length us, event | category | flops | bytes accessed | tf_op | source)
XLA Modules:
  0.0 137.3 jit_solution(5685725750526515950)
XLA Ops:
  8.8 6.3 %all-to-all-start = ((s32[4,1,5]{2,1,0:T(1,128)}), s32[4,1,5]{2,1,0:T(1,128)S(1)}, u32[]{:S(2)}, u32[]{:S(2)}) async-start(s32[4,1,5]{2,1,0:T(1,128)} %bitcast), calls=%async_computation | async-start | bytes 4096 | tf_op jit(solution)/shard_map/all_to_all | solution.py:110
  17.7 2.9 %all-to-all-done = s32[4,1,5]{2,1,0:T(1,128)S(1)} async-done(((s32[4,1,5]{2,1,0:T(1,128)}), s32[4,1,5]{2,1,0:T(1,128)S(1)}, u32[]{:S(2)}, u32[]{:S(2)}) %all-to-all-start) | async-done | bytes 112 | tf_op jit(solution)/shard_map/all_to_all | solution.py:110
  20.6 3.5 %all-to-all-start.1 = ((bf16[4,5,8,1024]{3,2,1,0:T(8,128)(2,1)}), bf16[4,5,8,1024]{3,2,1,0:T(8,128)(2,1)S(1)}, u32[]{:S(2)}, u32[]{:S(2)}) async-start(bf16[4,5,8,1024]{3,2,1,0:T(8,128)(2,1)} %bitcast.17), calls=%async_computation.1 | async-start | bytes 655360 | tf_op jit(solution)/shard_map/all_to_all | solution.py:103
  24.2 9.1 %all-to-all-done.1 = bf16[4,5,8,1024]{3,2,1,0:T(8,128)(2,1)S(1)} async-done(((bf16[4,5,8,1024]{3,2,1,0:T(8,128)(2,1)}), bf16[4,5,8,1024]{3,2,1,0:T(8,128)(2,1)S(1)}, u32[]{:S(2)}, u32[]{:S(2)}) %all-to-all-start.1) | async-done | bytes 327712 | tf_op jit(solution)/shard_map/all_to_all | solution.py:103
  34.7 27.0 %all-gather.2.cloned.1.call-done = bf16[16,64,1024]{2,1,0:T(8,128)(2,1)} async-done(((bf16[16,8,1024]{2,1,0:T(8,128)(2,1)}), bf16[16,64,1024]{2,1,0:T(8,128)(2,1)}) %all-gather.2.cloned.1.call-update) | async-done | bytes 2097168 | tf_op jit(solution)/shard_map/all_gather | solution.py:113
  61.7 2.2 %fusion.9 = f32[16,64]{1,0:T(8,128)S(1)} fusion(bf16[16,64,1024]{2,1,0:T(8,128)(2,1)} %all-gather.2.cloned.1.call-done), kind=kLoop, calls=%fused_computation.15 | loop fusion | flops 3144704 | bytes 2101248 | tf_op jit(solution)/shard_map/reduce_sum | solution.py:20
  64.0 2.1 %fusion.11 = bf16[16,64,1024]{2,1,0:T(8,128)(2,1)S(1)} fusion(bf16[16,64,1024]{2,1,0:T(8,128)(2,1)} %all-gather.2.cloned.1.call-done, f32[1024]{0:T(1024)S(1)} %copy-done.6, f32[16,64]{1,0:T(8,128)S(1)} %add_rsqrt_fusion), kind=kLoop, calls=%fused_computation.17 | loop fusion | flops 4194304 | bytes 4202496 | tf_op jit(solution)/shard_map/convert_element_type | solution.py:21
  66.1 4.7 %fusion.20 = bf16[1024,2048]{1,0:T(8,128)(2,1)S(1)} fusion(bf16[1024,1024]{1,0:T(8,128)(2,1)S(1)} %bitcast.64, bf16[1,1024,2048]{2,1,0:T(8,128)(2,1)S(1)} %copy-done.7), kind=kOutput, calls=%fused_computation.25 | convolution fusion | flops 4297064448 | bytes 10485760 | tf_op jit(solution)/shard_map/dot_general | solution.py:26
  71.8 3.7 %collective-permute-start.1 = (bf16[128,2048]{1,0:T(8,128)(2,1)}, bf16[128,2048]{1,0:T(8,128)(2,1)S(1)}, u32[]{:S(2)}, u32[]{:S(2)}) collective-permute-start(bf16[128,2048]{1,0:T(8,128)(2,1)} %slice.14), channel_id=1, source_target_pairs={{0,2},{2,4},{4,6},{1,3},{3,5},{5,7},{8,10},{10,12},{12,14},{9,11},... | collective-permute-start | bytes 1572872 | tf_op jit(solution)/shard_map/ppermute | solution.py:15
  75.4 4.7 %fusion.17 = bf16[1024,2048]{1,0:T(8,128)(2,1)S(1)} fusion(bf16[1024,1024]{1,0:T(8,128)(2,1)S(1)} %bitcast.65, bf16[1,1024,2048]{2,1,0:T(8,128)(2,1)S(1)} %copy-done.8), kind=kOutput, calls=%fused_computation.24 | convolution fusion | flops 4297064448 | bytes 10485760 | tf_op jit(solution)/shard_map/dot_general | solution.py:26
  81.1 1.3 copy-done.2
  82.4 3.6 %collective-permute-start = (bf16[128,2048]{1,0:T(8,128)(2,1)}, bf16[128,2048]{1,0:T(8,128)(2,1)S(1)}, u32[]{:S(2)}, u32[]{:S(2)}) collective-permute-start(bf16[128,2048]{1,0:T(8,128)(2,1)} %slice.15), channel_id=1, source_target_pairs={{0,2},{2,4},{4,6},{1,3},{3,5},{5,7},{8,10},{10,12},{12,14},{9,11},... | collective-permute-start | bytes 1572872 | tf_op jit(solution)/shard_map/ppermute | solution.py:15
  86.0 1.0 maximum_bitcast_fusion
  88.2 1.4 %copy.39 = bf16[128,8,16,128]{3,2,1,0:T(8,128)(2,1)S(1)} copy(bf16[128,8,16,128]{3,1,2,0:T(8,128)(2,1)S(1)} %bitcast.62) | data formatting | bytes 8388608
  89.7 3.2 %copy.26 = bf16[8,128,16,128]{3,1,2,0:T(8,128)(2,1)} copy(bf16[8,128,16,128]{3,2,1,0:T(8,128)(2,1)S(1)} %bitcast.56) | data formatting | bytes 8388608 | tf_op jit(solution)/shard_map/concatenate | solution.py:88
  92.8 1.4 %copy.37 = bf16[128,8,16,128]{3,2,1,0:T(8,128)(2,1)S(1)} copy(bf16[128,8,16,128]{3,1,2,0:T(8,128)(2,1)S(1)} %bitcast.61) | data formatting | bytes 8388608
  94.3 1.2 copy.28
  95.7 2.8 %collective-permute-done = bf16[128,2048]{1,0:T(8,128)(2,1)S(1)} collective-permute-done((bf16[128,2048]{1,0:T(8,128)(2,1)}, bf16[128,2048]{1,0:T(8,128)(2,1)S(1)}, u32[]{:S(2)}, u32[]{:S(2)}) %collective-permute-start) | collective-permute-done | bytes 524320 | tf_op jit(solution)/shard_map/ppermute | solution.py:15
  98.8 3.3 %fusion.1 = f32[9,16,64,128]{3,2,1,0:T(8,128)S(1)} fusion(bf16[8,128,16,128]{3,1,2,0:T(8,128)(2,1)S(1)} %copy.28, bf16[1,128,16,128]{3,1,2,0:T(8,128)(2,1)S(1)} %copy.27, bf16[9,64,16,128]{3,2,1,0:T(8,128)(2,1)S(1)} %bitcast.59), kind=kOutput, calls=%fused_computation.5 | convolution fusion | flops 304349184 | bytes 11796480 | tf_op jit(solution)/shard_map/wqhd,wkhd->whqk/dot_general | solution.py:35
  102.1 2.1 %copy-done.4 = f32[9,16,64,128]{3,2,1,0:T(8,128)} copy-done((f32[9,16,64,128]{3,2,1,0:T(8,128)}, f32[9,16,64,128]{3,2,1,0:T(8,128)S(1)}, u32[]{:S(2)}) %copy-start.4) | copy-done | bytes 4718616
  104.2 2.5 %fusion.51 = f32[9,16,64]{2,1,0:T(8,128)S(1)} fusion(f32[9,16,64,128]{3,2,1,0:T(8,128)S(1)} %fusion.1), kind=kOutput, calls=%fused_computation.71 | output fusion | flops 4718719 | bytes 4755456 | tf_op jit(solution)/shard_map/sub | solution.py:39
  106.7 19.5 %convert_bitcast_fusion = bf16[9,64,16,128]{3,1,2,0:T(8,128)(2,1)S(1)} fusion(bf16[8,128,16,128]{3,1,2,0:T(8,128)(2,1)} %copy.26, bf16[1,128,16,128]{3,1,2,0:T(8,128)(2,1)S(1)} %copy.25, f32[9,16,64]{2,1,0:T(8,128)S(1)} %fusion.51, f32[9,16,64,128]{3,2,1,0:T(8,128)} %copy-done.4), kind=kOutput, calls=%fused_computation.29 | convolution fusion | flops 318514304 | bytes 11833344 | tf_op jit(solution)/shard_map/whqk,wkhd->wqhd/dot_general | solution.py:41
  126.2 1.6 %copy.30 = bf16[9,64,16,128]{3,2,1,0:T(8,128)(2,1)S(1)} copy(bf16[9,64,16,128]{3,1,2,0:T(8,128)(2,1)S(1)} %convert_bitcast_fusion) | data formatting | bytes 4718592 | tf_op jit(solution)/shard_map/convert_element_type | solution.py:42
  128.5 2.0 %fusion.28 = bf16[1,512,2048]{2,1,0:T(8,128)(2,1)} fusion(bf16[576,2048]{1,0:T(8,128)(2,1)S(1)} %bitcast.60, pred[512]{0:T(512)(128)(4,1)S(1)} %fusion.44), kind=kLoop, calls=%fused_computation.33 | loop fusion | flops 1048576 | bytes 4194816 | tf_op jit(solution)/shard_map/broadcast_in_dim | solution.py:126
  (49 shorter events, 10.4 us)
Async XLA Ops:
  8.8 11.8 %all-to-all-start = ((s32[4,1,5]{2,1,0:T(1,128)}), s32[4,1,5]{2,1,0:T(1,128)S(1)}, u32[]{:S(2)}, u32[]{:S(2)}) async-start(s32[4,1,5]{2,1,0:T(1,128)} %bitcast), calls=%async_computation | async-start | bytes 4096 | tf_op jit(solution)/shard_map/all_to_all | solution.py:110
  16.2 47.8 %copy-start.6 = (f32[1024]{0:T(1024)S(1)}, f32[1024]{0:T(1024)}, u32[]{:S(2)}) copy-start(f32[1024]{0:T(1024)} %param.9) | copy-start | bytes 12292
  20.6 12.7 %all-to-all-start.1 = ((bf16[4,5,8,1024]{3,2,1,0:T(8,128)(2,1)}), bf16[4,5,8,1024]{3,2,1,0:T(8,128)(2,1)S(1)}, u32[]{:S(2)}, u32[]{:S(2)}) async-start(bf16[4,5,8,1024]{3,2,1,0:T(8,128)(2,1)} %bitcast.17), calls=%async_computation.1 | async-start | bytes 655360 | tf_op jit(solution)/shard_map/all_to_all | solution.py:103
  24.1 37.6 %all-gather.2.cloned.1.call-start = ((), (), s32[]{:S(2)}) async-start(), calls=%async_computation.2 | async-start | bytes 2359296 | tf_op jit(solution)/shard_map/all_gather | solution.py:113
  61.7 4.4 %copy-start.7 = (bf16[1,1024,2048]{2,1,0:T(8,128)(2,1)S(1)}, bf16[1,1024,2048]{2,1,0:T(8,128)(2,1)}, u32[]{:S(2)}) copy-start(bf16[1,1024,2048]{2,1,0:T(8,128)(2,1)} %param.7) | copy-start | bytes 12582916
  66.1 9.3 %copy-start.8 = (bf16[1,1024,2048]{2,1,0:T(8,128)(2,1)S(1)}, bf16[1,1024,2048]{2,1,0:T(8,128)(2,1)}, u32[]{:S(2)}) copy-start(bf16[1,1024,2048]{2,1,0:T(8,128)(2,1)} %param.8) | copy-start | bytes 12582916
  70.9 9.3 %copy-start = (bf16[1024,2048]{1,0:T(8,128)(2,1)}, bf16[1024,2048]{1,0:T(8,128)(2,1)S(1)}, u32[]{:S(2)}) copy-start(bf16[1024,2048]{1,0:T(8,128)(2,1)S(1)} %fusion.20) | copy-start | bytes 12582916
  71.8 14.3 %copy-start.5 = (bf16[1,512,2048]{2,1,0:T(8,128)(2,1)S(1)}, bf16[1,512,2048]{2,1,0:T(8,128)(2,1)}, u32[]{:S(2)}) copy-start(bf16[1,512,2048]{2,1,0:T(8,128)(2,1)} %param.6) | copy-start | bytes 6291460
  71.8 23.7 %collective-permute-start.1 = (bf16[128,2048]{1,0:T(8,128)(2,1)}, bf16[128,2048]{1,0:T(8,128)(2,1)S(1)}, u32[]{:S(2)}, u32[]{:S(2)}) collective-permute-start(bf16[128,2048]{1,0:T(8,128)(2,1)} %slice.14), channel_id=1, source_target_pairs={{0,2},{2,4},{4,6},{1,3},{3,5},{5,7},{8,10},{10,12},{12,14},{9,11},... | collective-permute-start | bytes 1572872 | tf_op jit(solution)/shard_map/ppermute | solution.py:15
  80.2 2.2 %copy-start.2 = (bf16[1024,2048]{1,0:T(8,128)(2,1)}, bf16[1024,2048]{1,0:T(8,128)(2,1)S(1)}, u32[]{:S(2)}) copy-start(bf16[1024,2048]{1,0:T(8,128)(2,1)S(1)} %fusion.17) | copy-start | bytes 12582916
  82.4 16.1 %collective-permute-start = (bf16[128,2048]{1,0:T(8,128)(2,1)}, bf16[128,2048]{1,0:T(8,128)(2,1)S(1)}, u32[]{:S(2)}, u32[]{:S(2)}) collective-permute-start(bf16[128,2048]{1,0:T(8,128)(2,1)} %slice.15), channel_id=1, source_target_pairs={{0,2},{2,4},{4,6},{1,3},{3,5},{5,7},{8,10},{10,12},{12,14},{9,11},... | collective-permute-start | bytes 1572872 | tf_op jit(solution)/shard_map/ppermute | solution.py:15
  86.0 2.2 %copy-start.3 = (bf16[1024,2048]{1,0:T(8,128)(2,1)S(1)}, bf16[1024,2048]{1,0:T(8,128)(2,1)}, u32[]{:S(2)}) copy-start(bf16[1024,2048]{1,0:T(8,128)(2,1)} %copy-done.2) | copy-start | bytes 12582916
  89.6 3.2 %copy-start.1 = (bf16[1024,2048]{1,0:T(8,128)(2,1)S(1)}, bf16[1024,2048]{1,0:T(8,128)(2,1)}, u32[]{:S(2)}) copy-start(bf16[1024,2048]{1,0:T(8,128)(2,1)} %copy-done) | copy-start | bytes 12582916
  102.1 2.1 %copy-start.4 = (f32[9,16,64,128]{3,2,1,0:T(8,128)}, f32[9,16,64,128]{3,2,1,0:T(8,128)S(1)}, u32[]{:S(2)}) copy-start(f32[9,16,64,128]{3,2,1,0:T(8,128)S(1)} %fusion.1) | copy-start | bytes 14155780
Sparse Core Ops, SparseCore 0:
  34.8 26.8 all-gather.1
where the time goes:
time: 138 us; the launch traced here: 137 us
  waiting for transfers between devices  41.9 us (30%)
  matrix products  32.7 us (24%)
  local copies, waits for them, and re-layouts  20.4 us (15%)
  starting transfers between devices  17.1 us (12%)
  between operations  13.7 us (10%)
  other arithmetic  11.6 us (8%)
    all_gather x1, waiting for transfers between devices, on_device(): routed = lax.all_gather(arranged, ('phase', 'mp'), axis=1, tiled=True)  27 us
    dot_general x1, matrix products, attend(): jnp.einsum('whqk,wkhd->wqhd', weights, value_four, preferred_element_type...  19.5 us
    unnamed x31, local copies, waits for them, and re-layouts  11.5 us
    dot_general x2, matrix products, project(): jnp.dot(flattened, weight, preferred_element_type=jnp.float32)  9.46 us
    all_to_all x1, waiting for transfers between devices, on_device(): lax.all_to_all(pack(selector, neighbour_states, shards, capacity), 'seq',...  9.08 us
    ppermute x2, starting transfers between devices, shifted(): return lax.ppermute(shard, axis, pairs)  7.23 us
    all_to_all x1, starting transfers between devices, on_device(): lax.all_to_all(sent_dest, 'seq', split_axis=0, concat_axis=0, tiled=True)  6.35 us
    all_to_all x1, starting transfers between devices, on_device(): lax.all_to_all(pack(selector, neighbour_states, shards, capacity), 'seq',...  3.45 us
  transfers between devices with their start and end apart: 5, of which 4 were waited for; matrix products, arithmetic and copies ran while one was open for 13% of the time, Pallas kernels for 0%

commit v1 on v0

--- a/solution.py
+++ b/solution.py
@@ -110,7 +110,12 @@
         lax.all_to_all(sent_dest, "seq", split_axis=0, concat_axis=0, tiled=True),
     )
     arranged = unpack(received, received_dest, own_index, per_shard)
-    routed = lax.all_gather(arranged, ("phase", "mp"), axis=1, tiled=True)
+    routed = jnp.concatenate(
+        lax.all_to_all(
+            jnp.stack([arranged] * lax.axis_size(("phase", "mp"))), ("phase", "mp"), 0, 0
+        ),
+        axis=1,
+    )
     neighbours = normalize(routed, enc_gain)
     key_mat = key_weight[0]
     value_mat = value_weight[0]

time: 138 us -> 122 us (0.88)
  blocking collectives: 0 us -> 29.2 us
  waiting for transfers between devices: 41.9 us -> 16.2 us
  between operations: 13.7 us -> 0.32 us
  other arithmetic: 11.6 us -> 8.25 us
  starting transfers between devices: 17.1 us -> 14.3 us
    all_to_all x0 -> x1, blocking collectives: none -> 29.2 us  [on_device(): lax.all_to_all(jnp.stack([arranged] * lax.axis_size(('phase', 'mp'))), ('...]
    all_gather x1 -> x0, waiting for transfers between devices: 27 us -> none  [on_device(): routed = lax.all_gather(arranged, ('phase', 'mp'), axis=1, tiled=True)]
    ppermute x2, starting transfers between devices: 7.23 us -> 4.5 us  [shifted(): return lax.ppermute(shard, axis, pairs)]
    reduce_sum x1, other arithmetic: 2.22 us -> 0.48 us  [normalize(): meansq = jnp.mean(states * states, axis=-1, keepdims=True)]
    convert_element_type x1, other arithmetic: 2.13 us -> 0.54 us  [normalize(): return (states * lax.rsqrt(meansq + 1e-06) * gain).astype(jnp.bfloat16)]
  transfers between devices with their start and end apart: 5 -> 4, of which waited for: 4 -> 3; matrix products, arithmetic and copies ran while one was open for 13% -> 14% of each run, Pallas kernels for 0% -> 0%
where the time goes in v1:
time: 122 us
  matrix products  32.7 us (27%)
  blocking collectives  29.2 us (24%)
  local copies, waits for them, and re-layouts  21.1 us (17%)
  waiting for transfers between devices  16.2 us (13%)
  starting transfers between devices  14.3 us (12%)
  other arithmetic  8.25 us (7%)
    all_to_all x1, blocking collectives, on_device(): lax.all_to_all(jnp.stack([arranged] * lax.axis_size(('phase', 'mp'))), ('...  29.2 us
    dot_general x1, matrix products, attend(): jnp.einsum('whqk,wkhd->wqhd', weights, value_four, preferred_element_type...  19.5 us
    unnamed x31, local copies, waits for them, and re-layouts  11.9 us
    dot_general x2, matrix products, project(): jnp.dot(flattened, weight, preferred_element_type=jnp.float32)  9.44 us
    all_to_all x1, waiting for transfers between devices, on_device(): lax.all_to_all(pack(selector, neighbour_states, shards, capacity), 'seq',...  9.13 us
    all_to_all x1, starting transfers between devices, on_device(): lax.all_to_all(sent_dest, 'seq', split_axis=0, concat_axis=0, tiled=True)  6.35 us
    ppermute x2, starting transfers between devices, shifted(): return lax.ppermute(shard, axis, pairs)  4.5 us
    ppermute x2, waiting for transfers between devices, shifted(): return lax.ppermute(shard, axis, pairs)  4.17 us
  transfers between devices with their start and end apart: 4, of which 3 were waited for; matrix products, arithmetic and copies ran while one was open for 14% of the time, Pallas kernels for 0%

profile of v1, /device:TPU:0, one launch (start us, length us, event | category | flops | bytes accessed | tf_op | source)
XLA Modules:
  0.0 122.0 jit_solution(542537540008947141)
XLA Ops:
  2.3 6.3 %all-to-all-start = ((s32[4,1,5]{2,1,0:T(1,128)}), s32[4,1,5]{2,1,0:T(1,128)S(1)}, u32[]{:S(2)}, u32[]{:S(2)}) async-start(s32[4,1,5]{2,1,0:T(1,128)} %bitcast), calls=%async_computation | async-start | bytes 4096 | tf_op jit(solution)/shard_map/all_to_all | solution.py:110
  8.7 1.0 pad.7
  11.1 2.9 %all-to-all-done = s32[4,1,5]{2,1,0:T(1,128)S(1)} async-done(((s32[4,1,5]{2,1,0:T(1,128)}), s32[4,1,5]{2,1,0:T(1,128)S(1)}, u32[]{:S(2)}, u32[]{:S(2)}) %all-to-all-start) | async-done | bytes 112 | tf_op jit(solution)/shard_map/all_to_all | solution.py:110
  14.1 3.5 %all-to-all-start.1 = ((bf16[4,5,8,1024]{3,2,1,0:T(8,128)(2,1)}), bf16[4,5,8,1024]{3,2,1,0:T(8,128)(2,1)S(1)}, u32[]{:S(2)}, u32[]{:S(2)}) async-start(bf16[4,5,8,1024]{3,2,1,0:T(8,128)(2,1)} %bitcast.18), calls=%async_computation.1 | async-start | bytes 655360 | tf_op jit(solution)/shard_map/all_to_all | solution.py:103
  17.7 9.1 %all-to-all-done.1 = bf16[4,5,8,1024]{3,2,1,0:T(8,128)(2,1)S(1)} async-done(((bf16[4,5,8,1024]{3,2,1,0:T(8,128)(2,1)}), bf16[4,5,8,1024]{3,2,1,0:T(8,128)(2,1)S(1)}, u32[]{:S(2)}, u32[]{:S(2)}) %all-to-all-start.1) | async-done | bytes 327712 | tf_op jit(solution)/shard_map/all_to_all | solution.py:103
  27.7 29.2 %all_to_all.16 = bf16[8,16,8,1024]{3,2,1,0:T(8,128)(2,1)S(1)} all-to-all(bf16[8,16,8,1024]{3,2,1,0:T(8,128)(2,1)S(1)} %stack.3), channel_id=1, replica_groups=mesh['phase'=4,'seq'=4,'mp'=2] {'phase','mp'}, dimensions={0} | all-to-all | bytes 4194304 | tf_op jit(solution)/shard_map/all_to_all | solution.py:114
  58.0 1.1 copy-done.7
  59.1 4.7 %fusion.20 = bf16[1024,2048]{1,0:T(8,128)(2,1)S(1)} fusion(bf16[1024,1024]{1,0:T(8,128)(2,1)S(1)} %bitcast.73, bf16[1,1024,2048]{2,1,0:T(8,128)(2,1)S(1)} %copy-done.7), kind=kOutput, calls=%fused_computation.25 | convolution fusion | flops 4297064448 | bytes 10485760 | tf_op jit(solution)/shard_map/dot_general | solution.py:26
  64.7 2.0 %collective-permute-start.1 = (bf16[128,2048]{1,0:T(8,128)(2,1)}, bf16[128,2048]{1,0:T(8,128)(2,1)S(1)}, u32[]{:S(2)}, u32[]{:S(2)}) collective-permute-start(bf16[128,2048]{1,0:T(8,128)(2,1)} %slice.14), channel_id=1, source_target_pairs={{0,2},{2,4},{4,6},{1,3},{3,5},{5,7},{8,10},{10,12},{12,14},{9,11},... | collective-permute-start | bytes 1572872 | tf_op jit(solution)/shard_map/ppermute | solution.py:15
  66.8 4.7 %fusion.17 = bf16[1024,2048]{1,0:T(8,128)(2,1)S(1)} fusion(bf16[1024,1024]{1,0:T(8,128)(2,1)S(1)} %bitcast.74, bf16[1,1024,2048]{2,1,0:T(8,128)(2,1)S(1)} %copy-done.8), kind=kOutput, calls=%fused_computation.24 | convolution fusion | flops 4297064448 | bytes 10485760 | tf_op jit(solution)/shard_map/dot_general | solution.py:26
  72.4 1.3 %copy-done.2 = bf16[1024,2048]{1,0:T(8,128)(2,1)} copy-done((bf16[1024,2048]{1,0:T(8,128)(2,1)}, bf16[1024,2048]{1,0:T(8,128)(2,1)S(1)}, u32[]{:S(2)}) %copy-start.2) | copy-done | bytes 4194328
  73.7 2.5 %collective-permute-start = (bf16[128,2048]{1,0:T(8,128)(2,1)}, bf16[128,2048]{1,0:T(8,128)(2,1)S(1)}, u32[]{:S(2)}, u32[]{:S(2)}) collective-permute-start(bf16[128,2048]{1,0:T(8,128)(2,1)} %slice.15), channel_id=1, source_target_pairs={{0,2},{2,4},{4,6},{1,3},{3,5},{5,7},{8,10},{10,12},{12,14},{9,11},... | collective-permute-start | bytes 1572872 | tf_op jit(solution)/shard_map/ppermute | solution.py:15
  76.2 1.0 maximum_bitcast_fusion
  78.4 1.4 %copy.41 = bf16[128,8,16,128]{3,2,1,0:T(8,128)(2,1)S(1)} copy(bf16[128,8,16,128]{3,1,2,0:T(8,128)(2,1)S(1)} %bitcast.71) | data formatting | bytes 8388608
  79.9 3.2 %copy.28 = bf16[8,128,16,128]{3,1,2,0:T(8,128)(2,1)} copy(bf16[8,128,16,128]{3,2,1,0:T(8,128)(2,1)S(1)} %bitcast.65) | data formatting | bytes 8388608 | tf_op jit(solution)/shard_map/concatenate | solution.py:88
  83.0 1.4 %copy.39 = bf16[128,8,16,128]{3,2,1,0:T(8,128)(2,1)S(1)} copy(bf16[128,8,16,128]{3,1,2,0:T(8,128)(2,1)S(1)} %bitcast.70) | data formatting | bytes 8388608
  84.5 1.2 copy.30
  85.9 4.2 %collective-permute-done = bf16[128,2048]{1,0:T(8,128)(2,1)S(1)} collective-permute-done((bf16[128,2048]{1,0:T(8,128)(2,1)}, bf16[128,2048]{1,0:T(8,128)(2,1)S(1)}, u32[]{:S(2)}, u32[]{:S(2)}) %collective-permute-start) | collective-permute-done | bytes 524320 | tf_op jit(solution)/shard_map/ppermute | solution.py:15
  90.4 3.3 %fusion.1 = f32[9,16,64,128]{3,2,1,0:T(8,128)S(1)} fusion(bf16[8,128,16,128]{3,1,2,0:T(8,128)(2,1)S(1)} %copy.30, bf16[1,128,16,128]{3,1,2,0:T(8,128)(2,1)S(1)} %copy.29, bf16[9,64,16,128]{3,2,1,0:T(8,128)(2,1)S(1)} %bitcast.68), kind=kOutput, calls=%fused_computation.3 | convolution fusion | flops 304349184 | bytes 11796480 | tf_op jit(solution)/shard_map/wqhd,wkhd->whqk/dot_general | solution.py:35
  93.7 2.1 %copy-done.4 = f32[9,16,64,128]{3,2,1,0:T(8,128)} copy-done((f32[9,16,64,128]{3,2,1,0:T(8,128)}, f32[9,16,64,128]{3,2,1,0:T(8,128)S(1)}, u32[]{:S(2)}) %copy-start.4) | copy-done | bytes 4718616
  95.8 2.5 %fusion.51 = f32[9,16,64]{2,1,0:T(8,128)S(1)} fusion(f32[9,16,64,128]{3,2,1,0:T(8,128)S(1)} %fusion.1), kind=kOutput, calls=%fused_computation.71 | output fusion | flops 4718719 | bytes 4755456 | tf_op jit(solution)/shard_map/sub | solution.py:39
  98.3 19.5 %convert_bitcast_fusion = bf16[9,64,16,128]{3,1,2,0:T(8,128)(2,1)S(1)} fusion(bf16[8,128,16,128]{3,1,2,0:T(8,128)(2,1)} %copy.28, bf16[1,128,16,128]{3,1,2,0:T(8,128)(2,1)S(1)} %copy.27, f32[9,16,64]{2,1,0:T(8,128)S(1)} %fusion.51, f32[9,16,64,128]{3,2,1,0:T(8,128)} %copy-done.4), kind=kOutput, calls=%fused_computation.29 | convolution fusion | flops 318514304 | bytes 11833344 | tf_op jit(solution)/shard_map/whqk,wkhd->wqhd/dot_general | solution.py:41
  117.8 1.6 %copy.32 = bf16[9,64,16,128]{3,2,1,0:T(8,128)(2,1)S(1)} copy(bf16[9,64,16,128]{3,1,2,0:T(8,128)(2,1)S(1)} %convert_bitcast_fusion) | data formatting | bytes 4718592 | tf_op jit(solution)/shard_map/convert_element_type | solution.py:42
  120.0 2.0 %fusion.28 = bf16[1,512,2048]{2,1,0:T(8,128)(2,1)} fusion(bf16[576,2048]{1,0:T(8,128)(2,1)S(1)} %bitcast.69, pred[512]{0:T(512)(128)(4,1)S(1)} %fusion.44), kind=kLoop, calls=%fused_computation.33 | loop fusion | flops 1048576 | bytes 4194816 | tf_op jit(solution)/shard_map/broadcast_in_dim | solution.py:131
  (48 shorter events, 9.9 us)
Async XLA Ops:
  2.3 11.8 %all-to-all-start = ((s32[4,1,5]{2,1,0:T(1,128)}), s32[4,1,5]{2,1,0:T(1,128)S(1)}, u32[]{:S(2)}, u32[]{:S(2)}) async-start(s32[4,1,5]{2,1,0:T(1,128)} %bitcast), calls=%async_computation | async-start | bytes 4096 | tf_op jit(solution)/shard_map/all_to_all | solution.py:110
  14.1 12.7 %all-to-all-start.1 = ((bf16[4,5,8,1024]{3,2,1,0:T(8,128)(2,1)}), bf16[4,5,8,1024]{3,2,1,0:T(8,128)(2,1)S(1)}, u32[]{:S(2)}, u32[]{:S(2)}) async-start(bf16[4,5,8,1024]{3,2,1,0:T(8,128)(2,1)} %bitcast.18), calls=%async_computation.1 | async-start | bytes 655360 | tf_op jit(solution)/shard_map/all_to_all | solution.py:103
  27.4 30.0 %copy-start.6 = (f32[1024]{0:T(1024)S(1)}, f32[1024]{0:T(1024)}, u32[]{:S(2)}) copy-start(f32[1024]{0:T(1024)} %param.9) | copy-start | bytes 12292
  56.9 2.2 %copy-start.7 = (bf16[1,1024,2048]{2,1,0:T(8,128)(2,1)S(1)}, bf16[1,1024,2048]{2,1,0:T(8,128)(2,1)}, u32[]{:S(2)}) copy-start(bf16[1,1024,2048]{2,1,0:T(8,128)(2,1)} %param.7) | copy-start | bytes 12582916
  59.1 7.7 %copy-start.8 = (bf16[1,1024,2048]{2,1,0:T(8,128)(2,1)S(1)}, bf16[1,1024,2048]{2,1,0:T(8,128)(2,1)}, u32[]{:S(2)}) copy-start(bf16[1,1024,2048]{2,1,0:T(8,128)(2,1)} %param.8) | copy-start | bytes 12582916
  63.8 7.7 %copy-start = (bf16[1024,2048]{1,0:T(8,128)(2,1)}, bf16[1024,2048]{1,0:T(8,128)(2,1)S(1)}, u32[]{:S(2)}) copy-start(bf16[1024,2048]{1,0:T(8,128)(2,1)S(1)} %fusion.20) | copy-start | bytes 12582916
  64.7 11.6 %copy-start.5 = (bf16[1,512,2048]{2,1,0:T(8,128)(2,1)S(1)}, bf16[1,512,2048]{2,1,0:T(8,128)(2,1)}, u32[]{:S(2)}) copy-start(bf16[1,512,2048]{2,1,0:T(8,128)(2,1)} %param.6) | copy-start | bytes 6291460
  64.7 21.0 %collective-permute-start.1 = (bf16[128,2048]{1,0:T(8,128)(2,1)}, bf16[128,2048]{1,0:T(8,128)(2,1)S(1)}, u32[]{:S(2)}, u32[]{:S(2)}) collective-permute-start(bf16[128,2048]{1,0:T(8,128)(2,1)} %slice.14), channel_id=1, source_target_pairs={{0,2},{2,4},{4,6},{1,3},{3,5},{5,7},{8,10},{10,12},{12,14},{9,11},... | collective-permute-start | bytes 1572872 | tf_op jit(solution)/shard_map/ppermute | solution.py:15
  71.5 2.2 %copy-start.2 = (bf16[1024,2048]{1,0:T(8,128)(2,1)}, bf16[1024,2048]{1,0:T(8,128)(2,1)S(1)}, u32[]{:S(2)}) copy-start(bf16[1024,2048]{1,0:T(8,128)(2,1)S(1)} %fusion.17) | copy-start | bytes 12582916
  73.7 16.4 %collective-permute-start = (bf16[128,2048]{1,0:T(8,128)(2,1)}, bf16[128,2048]{1,0:T(8,128)(2,1)S(1)}, u32[]{:S(2)}, u32[]{:S(2)}) collective-permute-start(bf16[128,2048]{1,0:T(8,128)(2,1)} %slice.15), channel_id=1, source_target_pairs={{0,2},{2,4},{4,6},{1,3},{3,5},{5,7},{8,10},{10,12},{12,14},{9,11},... | collective-permute-start | bytes 1572872 | tf_op jit(solution)/shard_map/ppermute | solution.py:15
  76.2 2.2 %copy-start.3 = (bf16[1024,2048]{1,0:T(8,128)(2,1)S(1)}, bf16[1024,2048]{1,0:T(8,128)(2,1)}, u32[]{:S(2)}) copy-start(bf16[1024,2048]{1,0:T(8,128)(2,1)} %copy-done.2) | copy-start | bytes 12582916
  79.8 3.2 %copy-start.1 = (bf16[1024,2048]{1,0:T(8,128)(2,1)S(1)}, bf16[1024,2048]{1,0:T(8,128)(2,1)}, u32[]{:S(2)}) copy-start(bf16[1024,2048]{1,0:T(8,128)(2,1)} %copy-done) | copy-start | bytes 12582916
  93.7 2.1 %copy-start.4 = (f32[9,16,64,128]{3,2,1,0:T(8,128)}, f32[9,16,64,128]{3,2,1,0:T(8,128)S(1)}, u32[]{:S(2)}) copy-start(f32[9,16,64,128]{3,2,1,0:T(8,128)S(1)} %fusion.1) | copy-start | bytes 14155780
